TPU v7x, 32 devices: a whole 2x2x4 slice. The times are simulated.
32 devices in a mesh: section: 2 (over core), dp: 4 (over y, x), tensor: 4 (over z).
Axes of the slice: x: 2, y: 2, z: 4, core: 2. Of those that a mesh axis runs over, the one named last changes fastest.
Arguments:
- section_input: bfloat16 [2, 512, 4096], P('section', 'dp'), may hold values from -60 to 60
- weights: bfloat16 [2, 4096, 4096], P('section', 'tensor', 'dp'), may hold values from -0.1875 to 0.1875
- gains: float32 [2, 4096], P('section'), may hold values from 0.1 to 1.9
- proj_seeds: int32 [2, 2], P('section'), may hold values from 0 to 99999
- out_grad: bfloat16 [512, 4096], P('dp'), may hold values from -0.75 to 0.75
- query_grads: bfloat16 [2, 256, 4096], P('section', 'dp', 'tensor'), may hold values from -0.017944336 to 0.017944336
Outputs:
- projected_grads: float32 [2, 2, 4096], P('section', None, 'tensor')
- scores: float32 [2, 256], P(None, 'dp')
All inputs are finite; a program needn't handle non-finite values.
Results may differ from a plain program's by a relative error of at most 0.033.
Values may be sent and summed in bfloat16 or wider, within the bound.
A program may use at most 64 MiB of HBM per device.

v0:
```python
import math
import jax
import jax.numpy as jnp
from jax import lax
from jax.sharding import PartitionSpec as P

R = 64
SEQS = 2
MICRO = 16
eps = 1e-05


def passed_along(value, axis, steps):
    count = lax.axis_size(axis)
    first, last = (max(0, -steps), min(count, count - steps))
    return lax.ppermute(value, axis, [(source, source + steps) for source in range(first, last)])


def sign_table(seed_value, row_count):
    row_index = lax.broadcasted_iota(jnp.int32, (row_count, R), 0)
    col_index = lax.broadcasted_iota(jnp.int32, (row_count, R), 1)
    mixing = row_index * 40503 + col_index * 9973 + seed_value * 7919 + 12345
    mixing = mixing ^ mixing >> 13
    mixing = mixing * 1274126177
    mixing = mixing ^ mixing >> 16
    parity = mixing >> 10 & 1
    return (jnp.where(parity == 1, 1.0, -1.0) * (1.0 / math.sqrt(row_count))).astype(jnp.bfloat16)


def take_rows(table, row_start):
    return lax.dynamic_slice_in_dim(table, row_start, MICRO, 0)


def body(section_input, weights, gains, proj_seeds, out_grad, query_grads):
    section_count = lax.axis_size("section")
    section_index = lax.axis_index("section")
    data_count = lax.axis_size("dp")
    data_index = lax.axis_index("dp")
    split_count = lax.axis_size("tensor")
    split_index = lax.axis_index("tensor")
    tok_rows = section_input.shape[1]
    feature_width = section_input.shape[2]
    slice_width = feature_width // split_count
    blocks = tok_rows // MICRO
    turn_count = section_count + blocks - 1
    own_start = split_index * slice_width
    gain_row = gains[0]
    hidden_in = section_input[0].astype(jnp.float32)
    radius = jnp.sqrt(jnp.mean(hidden_in * hidden_in, axis=1, keepdims=True) + eps)
    normed = hidden_in / radius
    lifted = (normed * gain_row).astype(jnp.bfloat16)
    weight_rows = lax.all_gather(weights[0], "dp", axis=1, tiled=True)
    lifted_own = lax.dynamic_slice_in_dim(lifted, own_start, slice_width, 1)
    partial_value = jnp.dot(lifted_own, weight_rows, preferred_element_type=jnp.float32)
    summed = lax.psum(partial_value.astype(jnp.bfloat16), "tensor").astype(jnp.float32)
    sigmoid_z = jax.nn.sigmoid(summed)
    slopes = sigmoid_z * (1.0 + summed * (1.0 - sigmoid_z))
    proj_in = sign_table(proj_seeds[0, 0], feature_width)
    proj_out = sign_table(proj_seeds[0, 1], feature_width)
    in_features = jnp.dot(lifted, proj_in, preferred_element_type=jnp.float32).astype(jnp.bfloat16)
    chain_depth = section_count - 1 - section_index
    at_top = section_index == section_count - 1

    def block_grad(operands):
        upstream, slope_rows, feature_rows, grad_sum = operands
        grad_pre = (upstream.astype(jnp.float32) * slope_rows).astype(jnp.bfloat16)
        out_features = jnp.dot(grad_pre, proj_out, preferred_element_type=jnp.float32).astype(
            jnp.bfloat16
        )
        grad_sum = grad_sum + lax.dot_general(
            feature_rows, out_features, (((0,), (0,)), ((), ())), preferred_element_type=jnp.float32
        )
        own_grads = lax.dot_general(
            grad_pre, weight_rows, (((1,), (1,)), ((), ())), preferred_element_type=jnp.float32
        ).astype(jnp.bfloat16)
        return (own_grads, grad_sum)

    def block_skip(operands):
        return (jnp.zeros((MICRO, slice_width), jnp.bfloat16), operands[3])

    def prepare(turn_index, upstream_in):
        block_index = turn_index.astype(jnp.int32) - chain_depth
        active = jnp.logical_and(block_index >= 0, block_index < blocks)
        row_start = jnp.clip(block_index, 0, blocks - 1) * MICRO
        top_rows = take_rows(out_grad, row_start)
        upstream = jnp.where(at_top, top_rows, upstream_in)
        return (active, row_start, upstream)

    def turn(turn_index, loop_state):
        incoming, grad_sum = loop_state
        active, row_start, upstream = prepare(turn_index, incoming)
        own_grads, grad_sum = lax.cond(
            active,
            block_grad,
            block_skip,
            (upstream, take_rows(slopes, row_start), take_rows(in_features, row_start), grad_sum),
        )
        full_grads = lax.all_gather(own_grads, "tensor", axis=1, tiled=True)

        def finish(operands):
            upstream_rows, grad_rows, normed_rows, radius_rows = operands
            scaled = grad_rows.astype(jnp.float32) * gain_row
            mean_dot = jnp.mean(scaled * normed_rows, axis=1, keepdims=True)
            return (
                upstream_rows.astype(jnp.float32) + (scaled - normed_rows * mean_dot) / radius_rows
            ).astype(jnp.bfloat16)

        def vacant(operands):
            return jnp.zeros((MICRO, feature_width), jnp.bfloat16)

        outgoing = lax.cond(
            active,
            finish,
            vacant,
            (upstream, full_grads, take_rows(normed, row_start), take_rows(radius, row_start)),
        )
        received = passed_along(outgoing, "section", -1)
        return (received, grad_sum)

    start_state = (jnp.zeros((MICRO, feature_width), jnp.bfloat16), jnp.zeros((R, R), jnp.float32))
    received, grad_sum = lax.fori_loop(0, turn_count, turn, start_state)
    flattened = grad_sum.reshape(R * R)
    piece_width = R * R // split_count
    own_part = lax.dynamic_slice_in_dim(flattened, split_index * piece_width, piece_width, 0)
    seq_index = data_index // (data_count // SEQS)
    seq_mask = (lax.broadcasted_iota(jnp.int32, (SEQS, 1), 0) == seq_index).astype(jnp.float32)
    per_seq = seq_mask * own_part[None, :]
    grads_all = lax.psum(per_seq, "dp")
    queries = query_grads[0].astype(jnp.float32)
    partial_scores = jnp.dot(grads_all, queries.T, precision=lax.Precision.HIGHEST)
    scores = lax.psum(partial_scores, ("section", "tensor"))
    return (grads_all[None], scores)


def solution(mesh):
    in_specs = (
        P("section", "dp", None),
        P("section", "tensor", "dp"),
        P("section", None),
        P("section", None),
        P("dp", None),
        P("section", "dp", "tensor"),
    )
    out_specs = (P("section", None, "tensor"), P(None, "dp"))
    return jax.shard_map(body, mesh=mesh, in_specs=in_specs, out_specs=out_specs, check_vma=False)
```

profile of v0, /device:TPU:1, one launch (start us, length us, event | category | flops | bytes accessed | tf_op | source)
XLA Modules:
  0.0 457.9 jit_solution(3057841927889815034)
XLA Ops:
  11.0 88.2 %all-gather.3.cloned.1.call-done = bf16[1,1024,4096]{2,1,0:T(8,128)(2,1)} async-done(((bf16[1,1024,1024]{2,1,0:T(8,128)(2,1)}), bf16[1,1024,4096]{2,1,0:T(8,128)(2,1)}) %all-gather.3.cloned.1.call-update) | async-done | bytes 8388624 | tf_op jit(solution)/shard_map/all_gather | solution.py:52
  99.3 5.7 %convolution_convert_fusion.2 = bf16[128,4096]{1,0:T(8,128)(2,1)} fusion(bf16[128,4096]{1,0:T(8,128)(2,1)S(1)} %get-tuple-element.421, s32[]{:T(128)S(6)} %select_n.44, bf16[1,1024,4096]{2,1,0:T(8,128)(2,1)} %all-gather.3.cloned.1.call-done), kind=kOutput, calls=%fused_computation.21 | convolution fusion | flops 1074266112 | bytes 9699332 | tf_op jit(solution)/shard_map/dot_general | solution.py:54
  111.4 45.8 %all-reduce.2.cloned.1.call-done = bf16[128,4096]{1,0:T(8,128)(2,1)} async-done(((bf16[128,4096]{1,0:T(8,128)(2,1)}), bf16[128,4096]{1,0:T(8,128)(2,1)}) %all-reduce.2.cloned.1.call-update) | async-done | bytes 1048592 | tf_op jit(solution)/shard_map/psum | solution.py:55
  159.8 263.6 %while.19 = (s32[]{:T(128)}, bf16[16,4096]{1,0:T(8,128)(2,1)S(1)}, f32[64,64]{1,0:T(8,128)}, s32[]{:T(128)}, pred[]{:T(512)}, /*index=5*/bf16[128,4096]{1,0:T(8,...) while((s32[]{:T(128)}, bf16[16,4096]{1,0:T(8,128)(2,1)S(1)}, ...), condition=%wide.region_8.9_spmd.clone, body=%wide.region_2.8_spmd.clone.sunk | while | flops 147674128 | bytes 13017286 | solution.py:121
  163.2 7.4 %conditional.6 = (bf16[16,1024]{1,0:T(8,128)(2,1)S(1)}, f32[64,64]{1,0:T(8,128)}) conditional(s32[]{:T(128)} %convert_element_type.134, f32[64,64]{1,0:T(8,128)} %get-tuple-element.548, (bf16[16,4096]{1,0:T(8,128)(2,1)S(1)}, f32[128,4096]{1,0:T(8,128)S(1)}, s32[]{:T(128)}, bf16[1024,4096]{1,0:T(8,128)(2,1)}, bf16[128,64]{1,0:T(8,128)(2,1)}, ...), branch_computations={%region_3.3_spmd, %region_4.4_spmd} | conditional | flops 143152128 | bytes 10310676 | solution.py:92
  170.6 10.4 %all_gather.13 = bf16[16,4096]{1,0:T(8,128)(2,1)S(1)} all-gather(bf16[16,1024]{1,0:T(8,128)(2,1)S(1)} %get-tuple-element.519), channel_id=1, replica_groups=mesh['section'=2,'dp'=4,'tensor'=4] {'tensor'}, dimensions={1}, use_global_device_ids=true | all-gather | bytes 163840 | tf_op jit(solution)/shard_map/while/body/eval_jaxpr/all_gather | solution.py:98
  189.0 7.4 %conditional.6 = (bf16[16,1024]{1,0:T(8,128)(2,1)S(1)}, f32[64,64]{1,0:T(8,128)}) conditional(s32[]{:T(128)} %convert_element_type.134, f32[64,64]{1,0:T(8,128)} %get-tuple-element.548, (bf16[16,4096]{1,0:T(8,128)(2,1)S(1)}, f32[128,4096]{1,0:T(8,128)S(1)}, s32[]{:T(128)}, bf16[1024,4096]{1,0:T(8,128)(2,1)}, bf16[128,64]{1,0:T(8,128)(2,1)}, ...), branch_computations={%region_3.3_spmd, %region_4.4_spmd} | conditional | flops 143152128 | bytes 10310676 | solution.py:92
  196.4 10.5 %all_gather.13 = bf16[16,4096]{1,0:T(8,128)(2,1)S(1)} all-gather(bf16[16,1024]{1,0:T(8,128)(2,1)S(1)} %get-tuple-element.519), channel_id=1, replica_groups=mesh['section'=2,'dp'=4,'tensor'=4] {'tensor'}, dimensions={1}, use_global_device_ids=true | all-gather | bytes 163840 | tf_op jit(solution)/shard_map/while/body/eval_jaxpr/all_gather | solution.py:98
  218.8 7.4 %conditional.6 = (bf16[16,1024]{1,0:T(8,128)(2,1)S(1)}, f32[64,64]{1,0:T(8,128)}) conditional(s32[]{:T(128)} %convert_element_type.134, f32[64,64]{1,0:T(8,128)} %get-tuple-element.548, (bf16[16,4096]{1,0:T(8,128)(2,1)S(1)}, f32[128,4096]{1,0:T(8,128)S(1)}, s32[]{:T(128)}, bf16[1024,4096]{1,0:T(8,128)(2,1)}, bf16[128,64]{1,0:T(8,128)(2,1)}, ...), branch_computations={%region_3.3_spmd, %region_4.4_spmd} | conditional | flops 143152128 | bytes 10310676 | solution.py:92
  226.2 10.5 %all_gather.13 = bf16[16,4096]{1,0:T(8,128)(2,1)S(1)} all-gather(bf16[16,1024]{1,0:T(8,128)(2,1)S(1)} %get-tuple-element.519), channel_id=1, replica_groups=mesh['section'=2,'dp'=4,'tensor'=4] {'tensor'}, dimensions={1}, use_global_device_ids=true | all-gather | bytes 163840 | tf_op jit(solution)/shard_map/while/body/eval_jaxpr/all_gather | solution.py:98
  248.5 7.4 %conditional.6 = (bf16[16,1024]{1,0:T(8,128)(2,1)S(1)}, f32[64,64]{1,0:T(8,128)}) conditional(s32[]{:T(128)} %convert_element_type.134, f32[64,64]{1,0:T(8,128)} %get-tuple-element.548, (bf16[16,4096]{1,0:T(8,128)(2,1)S(1)}, f32[128,4096]{1,0:T(8,128)S(1)}, s32[]{:T(128)}, bf16[1024,4096]{1,0:T(8,128)(2,1)}, bf16[128,64]{1,0:T(8,128)(2,1)}, ...), branch_computations={%region_3.3_spmd, %region_4.4_spmd} | conditional | flops 143152128 | bytes 10310676 | solution.py:92
  256.0 10.5 %all_gather.13 = bf16[16,4096]{1,0:T(8,128)(2,1)S(1)} all-gather(bf16[16,1024]{1,0:T(8,128)(2,1)S(1)} %get-tuple-element.519), channel_id=1, replica_groups=mesh['section'=2,'dp'=4,'tensor'=4] {'tensor'}, dimensions={1}, use_global_device_ids=true | all-gather | bytes 163840 | tf_op jit(solution)/shard_map/while/body/eval_jaxpr/all_gather | solution.py:98
  278.2 7.4 %conditional.6 = (bf16[16,1024]{1,0:T(8,128)(2,1)S(1)}, f32[64,64]{1,0:T(8,128)}) conditional(s32[]{:T(128)} %convert_element_type.134, f32[64,64]{1,0:T(8,128)} %get-tuple-element.548, (bf16[16,4096]{1,0:T(8,128)(2,1)S(1)}, f32[128,4096]{1,0:T(8,128)S(1)}, s32[]{:T(128)}, bf16[1024,4096]{1,0:T(8,128)(2,1)}, bf16[128,64]{1,0:T(8,128)(2,1)}, ...), branch_computations={%region_3.3_spmd, %region_4.4_spmd} | conditional | flops 143152128 | bytes 10310676 | solution.py:92
  285.7 10.5 %all_gather.13 = bf16[16,4096]{1,0:T(8,128)(2,1)S(1)} all-gather(bf16[16,1024]{1,0:T(8,128)(2,1)S(1)} %get-tuple-element.519), channel_id=1, replica_groups=mesh['section'=2,'dp'=4,'tensor'=4] {'tensor'}, dimensions={1}, use_global_device_ids=true | all-gather | bytes 163840 | tf_op jit(solution)/shard_map/while/body/eval_jaxpr/all_gather | solution.py:98
  308.0 7.4 %conditional.6 = (bf16[16,1024]{1,0:T(8,128)(2,1)S(1)}, f32[64,64]{1,0:T(8,128)}) conditional(s32[]{:T(128)} %convert_element_type.134, f32[64,64]{1,0:T(8,128)} %get-tuple-element.548, (bf16[16,4096]{1,0:T(8,128)(2,1)S(1)}, f32[128,4096]{1,0:T(8,128)S(1)}, s32[]{:T(128)}, bf16[1024,4096]{1,0:T(8,128)(2,1)}, bf16[128,64]{1,0:T(8,128)(2,1)}, ...), branch_computations={%region_3.3_spmd, %region_4.4_spmd} | conditional | flops 143152128 | bytes 10310676 | solution.py:92
  315.4 10.5 %all_gather.13 = bf16[16,4096]{1,0:T(8,128)(2,1)S(1)} all-gather(bf16[16,1024]{1,0:T(8,128)(2,1)S(1)} %get-tuple-element.519), channel_id=1, replica_groups=mesh['section'=2,'dp'=4,'tensor'=4] {'tensor'}, dimensions={1}, use_global_device_ids=true | all-gather | bytes 163840 | tf_op jit(solution)/shard_map/while/body/eval_jaxpr/all_gather | solution.py:98
  337.7 7.4 %conditional.6 = (bf16[16,1024]{1,0:T(8,128)(2,1)S(1)}, f32[64,64]{1,0:T(8,128)}) conditional(s32[]{:T(128)} %convert_element_type.134, f32[64,64]{1,0:T(8,128)} %get-tuple-element.548, (bf16[16,4096]{1,0:T(8,128)(2,1)S(1)}, f32[128,4096]{1,0:T(8,128)S(1)}, s32[]{:T(128)}, bf16[1024,4096]{1,0:T(8,128)(2,1)}, bf16[128,64]{1,0:T(8,128)(2,1)}, ...), branch_computations={%region_3.3_spmd, %region_4.4_spmd} | conditional | flops 143152128 | bytes 10310676 | solution.py:92
  345.1 10.5 %all_gather.13 = bf16[16,4096]{1,0:T(8,128)(2,1)S(1)} all-gather(bf16[16,1024]{1,0:T(8,128)(2,1)S(1)} %get-tuple-element.519), channel_id=1, replica_groups=mesh['section'=2,'dp'=4,'tensor'=4] {'tensor'}, dimensions={1}, use_global_device_ids=true | all-gather | bytes 163840 | tf_op jit(solution)/shard_map/while/body/eval_jaxpr/all_gather | solution.py:98
  367.4 7.4 %conditional.6 = (bf16[16,1024]{1,0:T(8,128)(2,1)S(1)}, f32[64,64]{1,0:T(8,128)}) conditional(s32[]{:T(128)} %convert_element_type.134, f32[64,64]{1,0:T(8,128)} %get-tuple-element.548, (bf16[16,4096]{1,0:T(8,128)(2,1)S(1)}, f32[128,4096]{1,0:T(8,128)S(1)}, s32[]{:T(128)}, bf16[1024,4096]{1,0:T(8,128)(2,1)}, bf16[128,64]{1,0:T(8,128)(2,1)}, ...), branch_computations={%region_3.3_spmd, %region_4.4_spmd} | conditional | flops 143152128 | bytes 10310676 | solution.py:92
  374.9 10.5 %all_gather.13 = bf16[16,4096]{1,0:T(8,128)(2,1)S(1)} all-gather(bf16[16,1024]{1,0:T(8,128)(2,1)S(1)} %get-tuple-element.519), channel_id=1, replica_groups=mesh['section'=2,'dp'=4,'tensor'=4] {'tensor'}, dimensions={1}, use_global_device_ids=true | all-gather | bytes 163840 | tf_op jit(solution)/shard_map/while/body/eval_jaxpr/all_gather | solution.py:98
  397.2 10.5 %all_gather.13 = bf16[16,4096]{1,0:T(8,128)(2,1)S(1)} all-gather(bf16[16,1024]{1,0:T(8,128)(2,1)S(1)} %get-tuple-element.519), channel_id=1, replica_groups=mesh['section'=2,'dp'=4,'tensor'=4] {'tensor'}, dimensions={1}, use_global_device_ids=true | all-gather | bytes 163840 | tf_op jit(solution)/shard_map/while/body/eval_jaxpr/all_gather | solution.py:98
  407.7 14.8 %collective-permute-start = (bf16[16,4096]{1,0:T(8,128)(2,1)S(1)}, bf16[16,4096]{1,0:T(8,128)(2,1)S(1)}, u32[]{:S(2)}, u32[]{:S(2)}) collective-permute-start(bf16[16,4096]{1,0:T(8,128)(2,1)S(1)} %get-tuple-element.588), channel_id=1, source_target_pairs={{16,0},{17,1},{18,2},{19,3},{20,4},{21,5},{22,6},{23,7},{24,8},{25... | collective-permute-start | bytes 393224 | tf_op jit(solution)/shard_map/while/body/eval_jaxpr/ppermute | solution.py:16
  425.0 7.8 %psum.22 = f32[2,1024]{1,0:T(2,128)S(1)} all-reduce(f32[2,1024]{1,0:T(2,128)S(1)} %broadcast_multiply_fusion.1), channel_id=1, replica_groups=mesh['section'=2,'dp'=4,'tensor'=4] {'dp'}, use_global_device_ids=true, to_apply=%region_9.10 | all-reduce | flops 2048 | bytes 16384 | tf_op jit(solution)/shard_map/psum | solution.py:128
  433.0 18.1 %psum.23 = f32[2,64]{1,0:T(2,128)} all-reduce(f32[2,64]{1,0:T(2,128)S(1)} %fusion.32), channel_id=1, replica_groups=mesh['section'=2,'dp'=4,'tensor'=4] {'section','tensor'}, use_global_device_ids=true, to_apply=%region_10.11 | all-reduce | flops 128 | bytes 1024 | tf_op jit(solution)/shard_map/psum | solution.py:131
  (143 shorter events, 186.1 us)
Async XLA Ops:
  7.2 425.6 %copy-start = (bf16[1,64,1024]{2,1,0:T(8,128)(2,1)S(1)}, bf16[1,64,1024]{2,1,0:T(8,128)(2,1)}, u32[]{:S(2)}) copy-start(bf16[1,64,1024]{2,1,0:T(8,128)(2,1)} %param.17) | copy-start | bytes 393220
  7.2 2.1 copy-start.2
  7.2 92.1 %all-gather.3.cloned.1.call-start = ((), (), s32[]{:S(2)}) async-start(), calls=%async_computation.1 | async-start | bytes 10485760 | tf_op jit(solution)/shard_map/all_gather | solution.py:52
  7.9 149.3 %all-reduce.2.cloned.1.call-start = ((), (), s32[]{:S(2)}) async-start(), calls=%async_computation | async-start | bytes 2097152 | tf_op jit(solution)/shard_map/psum | solution.py:55
  99.3 5.7 %copy-start.4 = (s32[1,2]{1,0:T(1,128)S(1)}, s32[1,2]{1,0:T(1,128)}, u32[]{:S(2)}) copy-start(s32[1,2]{1,0:T(1,128)} %param.15) | copy-start | bytes 28
  163.2 17.9 %copy-start.5 = (f32[128,1]{0,1:T(1,128)S(1)}, f32[128,1]{0,1:T(1,128)}, u32[]{:S(2)}) copy-start(f32[128,1]{0,1:T(1,128)} %get-tuple-element.578) | copy-start | bytes 1540 | tf_op jit(solution)/shard_map/while
  183.4 2.3 collective-permute-start
  189.0 17.9 %copy-start.5 = (f32[128,1]{0,1:T(1,128)S(1)}, f32[128,1]{0,1:T(1,128)}, u32[]{:S(2)}) copy-start(f32[128,1]{0,1:T(1,128)} %get-tuple-element.578) | copy-start | bytes 1540 | tf_op jit(solution)/shard_map/while
  209.3 6.2 %collective-permute-start = (bf16[16,4096]{1,0:T(8,128)(2,1)S(1)}, bf16[16,4096]{1,0:T(8,128)(2,1)S(1)}, u32[]{:S(2)}, u32[]{:S(2)}) collective-permute-start(bf16[16,4096]{1,0:T(8,128)(2,1)S(1)} %get-tuple-element.588), channel_id=1, source_target_pairs={{16,0},{17,1},{18,2},{19,3},{20,4},{21,5},{22,6},{23,7},{24,8},{25... | collective-permute-start | bytes 393224 | tf_op jit(solution)/shard_map/while/body/eval_jaxpr/ppermute | solution.py:16
  218.8 17.9 %copy-start.5 = (f32[128,1]{0,1:T(1,128)S(1)}, f32[128,1]{0,1:T(1,128)}, u32[]{:S(2)}) copy-start(f32[128,1]{0,1:T(1,128)} %get-tuple-element.578) | copy-start | bytes 1540 | tf_op jit(solution)/shard_map/while
  239.1 6.2 %collective-permute-start = (bf16[16,4096]{1,0:T(8,128)(2,1)S(1)}, bf16[16,4096]{1,0:T(8,128)(2,1)S(1)}, u32[]{:S(2)}, u32[]{:S(2)}) collective-permute-start(bf16[16,4096]{1,0:T(8,128)(2,1)S(1)} %get-tuple-element.588), channel_id=1, source_target_pairs={{16,0},{17,1},{18,2},{19,3},{20,4},{21,5},{22,6},{23,7},{24,8},{25... | collective-permute-start | bytes 393224 | tf_op jit(solution)/shard_map/while/body/eval_jaxpr/ppermute | solution.py:16
  248.5 17.9 %copy-start.5 = (f32[128,1]{0,1:T(1,128)S(1)}, f32[128,1]{0,1:T(1,128)}, u32[]{:S(2)}) copy-start(f32[128,1]{0,1:T(1,128)} %get-tuple-element.578) | copy-start | bytes 1540 | tf_op jit(solution)/shard_map/while
  268.8 6.1 %collective-permute-start = (bf16[16,4096]{1,0:T(8,128)(2,1)S(1)}, bf16[16,4096]{1,0:T(8,128)(2,1)S(1)}, u32[]{:S(2)}, u32[]{:S(2)}) collective-permute-start(bf16[16,4096]{1,0:T(8,128)(2,1)S(1)} %get-tuple-element.588), channel_id=1, source_target_pairs={{16,0},{17,1},{18,2},{19,3},{20,4},{21,5},{22,6},{23,7},{24,8},{25... | collective-permute-start | bytes 393224 | tf_op jit(solution)/shard_map/while/body/eval_jaxpr/ppermute | solution.py:16
  278.2 17.9 %copy-start.5 = (f32[128,1]{0,1:T(1,128)S(1)}, f32[128,1]{0,1:T(1,128)}, u32[]{:S(2)}) copy-start(f32[128,1]{0,1:T(1,128)} %get-tuple-element.578) | copy-start | bytes 1540 | tf_op jit(solution)/shard_map/while
  298.5 6.1 %collective-permute-start = (bf16[16,4096]{1,0:T(8,128)(2,1)S(1)}, bf16[16,4096]{1,0:T(8,128)(2,1)S(1)}, u32[]{:S(2)}, u32[]{:S(2)}) collective-permute-start(bf16[16,4096]{1,0:T(8,128)(2,1)S(1)} %get-tuple-element.588), channel_id=1, source_target_pairs={{16,0},{17,1},{18,2},{19,3},{20,4},{21,5},{22,6},{23,7},{24,8},{25... | collective-permute-start | bytes 393224 | tf_op jit(solution)/shard_map/while/body/eval_jaxpr/ppermute | solution.py:16
  308.0 17.9 %copy-start.5 = (f32[128,1]{0,1:T(1,128)S(1)}, f32[128,1]{0,1:T(1,128)}, u32[]{:S(2)}) copy-start(f32[128,1]{0,1:T(1,128)} %get-tuple-element.578) | copy-start | bytes 1540 | tf_op jit(solution)/shard_map/while
  328.3 6.1 %collective-permute-start = (bf16[16,4096]{1,0:T(8,128)(2,1)S(1)}, bf16[16,4096]{1,0:T(8,128)(2,1)S(1)}, u32[]{:S(2)}, u32[]{:S(2)}) collective-permute-start(bf16[16,4096]{1,0:T(8,128)(2,1)S(1)} %get-tuple-element.588), channel_id=1, source_target_pairs={{16,0},{17,1},{18,2},{19,3},{20,4},{21,5},{22,6},{23,7},{24,8},{25... | collective-permute-start | bytes 393224 | tf_op jit(solution)/shard_map/while/body/eval_jaxpr/ppermute | solution.py:16
  337.7 17.9 %copy-start.5 = (f32[128,1]{0,1:T(1,128)S(1)}, f32[128,1]{0,1:T(1,128)}, u32[]{:S(2)}) copy-start(f32[128,1]{0,1:T(1,128)} %get-tuple-element.578) | copy-start | bytes 1540 | tf_op jit(solution)/shard_map/while
  358.0 6.1 %collective-permute-start = (bf16[16,4096]{1,0:T(8,128)(2,1)S(1)}, bf16[16,4096]{1,0:T(8,128)(2,1)S(1)}, u32[]{:S(2)}, u32[]{:S(2)}) collective-permute-start(bf16[16,4096]{1,0:T(8,128)(2,1)S(1)} %get-tuple-element.588), channel_id=1, source_target_pairs={{16,0},{17,1},{18,2},{19,3},{20,4},{21,5},{22,6},{23,7},{24,8},{25... | collective-permute-start | bytes 393224 | tf_op jit(solution)/shard_map/while/body/eval_jaxpr/ppermute | solution.py:16
  367.4 17.9 %copy-start.5 = (f32[128,1]{0,1:T(1,128)S(1)}, f32[128,1]{0,1:T(1,128)}, u32[]{:S(2)}) copy-start(f32[128,1]{0,1:T(1,128)} %get-tuple-element.578) | copy-start | bytes 1540 | tf_op jit(solution)/shard_map/while
  387.6 6.2 %collective-permute-start = (bf16[16,4096]{1,0:T(8,128)(2,1)S(1)}, bf16[16,4096]{1,0:T(8,128)(2,1)S(1)}, u32[]{:S(2)}, u32[]{:S(2)}) collective-permute-start(bf16[16,4096]{1,0:T(8,128)(2,1)S(1)} %get-tuple-element.588), channel_id=1, source_target_pairs={{16,0},{17,1},{18,2},{19,3},{20,4},{21,5},{22,6},{23,7},{24,8},{25... | collective-permute-start | bytes 393224 | tf_op jit(solution)/shard_map/while/body/eval_jaxpr/ppermute | solution.py:16
  397.1 10.5 %copy-start.5 = (f32[128,1]{0,1:T(1,128)S(1)}, f32[128,1]{0,1:T(1,128)}, u32[]{:S(2)}) copy-start(f32[128,1]{0,1:T(1,128)} %get-tuple-element.578) | copy-start | bytes 1540 | tf_op jit(solution)/shard_map/while
  407.7 15.8 %collective-permute-start = (bf16[16,4096]{1,0:T(8,128)(2,1)S(1)}, bf16[16,4096]{1,0:T(8,128)(2,1)S(1)}, u32[]{:S(2)}, u32[]{:S(2)}) collective-permute-start(bf16[16,4096]{1,0:T(8,128)(2,1)S(1)} %get-tuple-element.588), channel_id=1, source_target_pairs={{16,0},{17,1},{18,2},{19,3},{20,4},{21,5},{22,6},{23,7},{24,8},{25... | collective-permute-start | bytes 393224 | tf_op jit(solution)/shard_map/while/body/eval_jaxpr/ppermute | solution.py:16
  432.8 18.3 %copy-start.3 = (f32[2,1024]{1,0:T(2,128)}, f32[2,1024]{1,0:T(2,128)S(1)}, u32[]{:S(2)}) copy-start(f32[2,1024]{1,0:T(2,128)S(1)} %psum.22) | copy-start | bytes 24580
  (1 other events, 1.3 us)
Sparse Core Ops, SparseCore 0:
  9.9 89.3 all-gather.2
  105.1 52.1 all-reduce.1
where the time goes:
time: 461 us; the launch traced here: 458 us
  waiting for transfers between devices  143 us (31%)
  blocking collectives  120 us (26%)
  matrix products  67.3 us (15%)
  other arithmetic  54.6 us (12%)
  starting transfers between devices  52.6 us (11%)
  between operations  15.4 us (3%)
    all_gather x9, blocking collectives, turn(): full_grads = lax.all_gather(own_grads, 'tensor', axis=1, tiled=True)  94.2 us
    all_gather x1, waiting for transfers between devices, body(): weight_rows = lax.all_gather(weights[0], 'dp', axis=1, tiled=True)  88.2 us
    ppermute x9, starting transfers between devices, passed_along(): lax.ppermute(value, axis, [(source, source + steps) for source in range(f...  52.5 us
    psum x1, waiting for transfers between devices, body(): lax.psum(partial_value.astype(jnp.bfloat16), 'tensor').astype(jnp.float32)  45.8 us
    dot_general x8, matrix products, block_grad(): lax.dot_general(grad_pre, weight_rows, (((1,), (1,)), ((), ())), preferre...  45.2 us
    convert_element_type x9, other arithmetic, sign_table(): (jnp.where(parity == 1, 1.0, -1.0) * (1.0 / math.sqrt(row_count))).astype...  21 us
    psum x1, blocking collectives, body(): scores = lax.psum(partial_scores, ('section', 'tensor'))  18.1 us
    dot_general x8, matrix products, block_grad(): lax.dot_general(feature_rows, out_features, (((0,), (0,)), ((), ())), pre...  14.2 us
  transfers between devices with their start and end apart: 11, of which 11 were waited for; matrix products, arithmetic and copies ran while one was open for 2% of the time, Pallas kernels for 0%

commit v1 on v0

--- a/solution.py
+++ b/solution.py
@@ -52,7 +52,9 @@
     weight_rows = lax.all_gather(weights[0], "dp", axis=1, tiled=True)
     lifted_own = lax.dynamic_slice_in_dim(lifted, own_start, slice_width, 1)
     partial_value = jnp.dot(lifted_own, weight_rows, preferred_element_type=jnp.float32)
-    summed = lax.psum(partial_value.astype(jnp.bfloat16), "tensor").astype(jnp.float32)
+    summed = jnp.sum(lax.all_gather(partial_value.astype(jnp.bfloat16), "tensor"), axis=0).astype(
+        jnp.float32
+    )
     sigmoid_z = jax.nn.sigmoid(summed)
     slopes = sigmoid_z * (1.0 + summed * (1.0 - sigmoid_z))
     proj_in = sign_table(proj_seeds[0, 0], feature_width)

time: 461 us -> 504 us (1.093)
  waiting for transfers between devices: 143 us -> 174 us
  local copies, waits for them, and re-layouts: 3.93 us -> 14.1 us
    all_gather x0 -> x1, waiting for transfers between devices: none -> 76.4 us  [body(): lax.all_gather(partial_value.astype(jnp.bfloat16), 'tensor')]
    psum x1 -> x0, waiting for transfers between devices: 45.8 us -> none  [body(): lax.psum(partial_value.astype(jnp.bfloat16), 'tensor').astype(jnp.float32)]
    while x18, local copies, waits for them, and re-layouts: 0.04 us -> 5.39 us
  transfers between devices with their start and end apart: 11 -> 11, of which waited for: 11 -> 11; matrix products, arithmetic and copies ran while one was open for 2% -> 1% of each run, Pallas kernels for 0% -> 0%
where the time goes in v1:
time: 504 us; the launch traced here: 501 us
  waiting for transfers between devices  174 us (35%)
  blocking collectives  121 us (24%)
  matrix products  66.6 us (13%)
  other arithmetic  55.2 us (11%)
  starting transfers between devices  53.6 us (11%)
  between operations  15.4 us (3%)
  local copies, waits for them, and re-layouts  14.1 us (3%)
    all_gather x9, blocking collectives, turn(): full_grads = lax.all_gather(own_grads, 'tensor', axis=1, tiled=True)  96.4 us
    all_gather x1, waiting for transfers between devices, body(): weight_rows = lax.all_gather(weights[0], 'dp', axis=1, tiled=True)  88.3 us
    all_gather x1, waiting for transfers between devices, body(): lax.all_gather(partial_value.astype(jnp.bfloat16), 'tensor')  76.4 us
    ppermute x9, starting transfers between devices, passed_along(): lax.ppermute(value, axis, [(source, source + steps) for source in range(f...  53.5 us
    dot_general x8, matrix products, block_grad(): lax.dot_general(grad_pre, weight_rows, (((1,), (1,)), ((), ())), preferre...  45.2 us
    convert_element_type x9, other arithmetic, sign_table(): (jnp.where(parity == 1, 1.0, -1.0) * (1.0 / math.sqrt(row_count))).astype...  21.1 us
    psum x1, blocking collectives, body(): scores = lax.psum(partial_scores, ('section', 'tensor'))  17 us
    dot_general x8, matrix products, block_grad(): lax.dot_general(feature_rows, out_features, (((0,), (0,)), ((), ())), pre...  14.2 us
  transfers between devices with their start and end apart: 11, of which 11 were waited for; matrix products, arithmetic and copies ran while one was open for 1% of the time, Pallas kernels for 0%

profile of v1, /device:TPU:1, one launch (start us, length us, event | category | flops | bytes accessed | tf_op | source)
XLA Modules:
  0.0 500.9 jit_solution(8214340285332486690)
XLA Ops:
  11.0 88.3 %all-gather.5.cloned.1.call-done = bf16[1,1024,4096]{2,1,0:T(8,128)(2,1)} async-done(((bf16[1,1024,1024]{2,1,0:T(8,128)(2,1)}), bf16[1,1024,4096]{2,1,0:T(8,128)(2,1)}) %all-gather.5.cloned.1.call-update) | async-done | bytes 8388624 | tf_op jit(solution)/shard_map/all_gather | solution.py:52
  99.3 5.6 %convolution_convert_fusion.2 = bf16[128,4096]{1,0:T(8,128)(2,1)} fusion(bf16[128,4096]{1,0:T(8,128)(2,1)S(1)} %get-tuple-element.421, s32[]{:T(128)S(6)} %select_n.44, bf16[1,1024,4096]{2,1,0:T(8,128)(2,1)} %all-gather.5.cloned.1.call-done), kind=kOutput, calls=%fused_computation.21 | convolution fusion | flops 1074266112 | bytes 9699332 | tf_op jit(solution)/shard_map/dot_general | solution.py:54
  109.5 76.4 %all-gather.7.cloned.1.call-done = bf16[512,4096]{1,0:T(8,128)(2,1)} async-done(((bf16[128,4096]{1,0:T(8,128)(2,1)}), bf16[512,4096]{1,0:T(8,128)(2,1)}) %all-gather.7.cloned.1.call-update) | async-done | bytes 4194320 | tf_op jit(solution)/shard_map/all_gather | solution.py:55
  190.3 277.1 %while.19 = (s32[]{:T(128)}, bf16[16,4096]{1,0:T(8,128)(2,1)S(1)}, f32[64,64]{1,0:T(8,128)}, s32[]{:T(128)}, pred[]{:T(512)}, /*index=5*/bf16[128,4096]{1,0:T(8,...) while((s32[]{:T(128)}, bf16[16,4096]{1,0:T(8,128)(2,1)S(1)}, ...), condition=%wide.region_8.9_spmd.clone, body=%wide.region_2.8_spmd.clone.sunk | while | flops 147674128 | bytes 13146310 | solution.py:123
  193.6 7.4 %conditional.6 = (bf16[16,1024]{1,0:T(8,128)(2,1)S(1)}, f32[64,64]{1,0:T(8,128)}) conditional(s32[]{:T(128)} %convert_element_type.136, f32[64,64]{1,0:T(8,128)} %get-tuple-element.548, (bf16[16,4096]{1,0:T(8,128)(2,1)S(1)}, f32[128,4096]{1,0:T(8,128)S(1)}, s32[]{:T(128)}, bf16[1024,4096]{1,0:T(8,128)(2,1)}, bf16[128,64]{1,0:T(8,128)(2,1)}, ...), branch_computations={%region_3.3_spmd, %region_4.4_spmd} | conditional | flops 143152128 | bytes 10310676 | solution.py:94
  201.7 10.7 %all_gather.21 = bf16[16,4096]{1,0:T(8,128)(2,1)S(1)} all-gather(bf16[16,1024]{1,0:T(8,128)(2,1)} %copy-done.2), channel_id=1, replica_groups=mesh['section'=2,'dp'=4,'tensor'=4] {'tensor'}, dimensions={1}, use_global_device_ids=true | all-gather | bytes 163840 | tf_op jit(solution)/shard_map/while/body/eval_jaxpr/all_gather | solution.py:100
  220.8 7.4 %conditional.6 = (bf16[16,1024]{1,0:T(8,128)(2,1)S(1)}, f32[64,64]{1,0:T(8,128)}) conditional(s32[]{:T(128)} %convert_element_type.136, f32[64,64]{1,0:T(8,128)} %get-tuple-element.548, (bf16[16,4096]{1,0:T(8,128)(2,1)S(1)}, f32[128,4096]{1,0:T(8,128)S(1)}, s32[]{:T(128)}, bf16[1024,4096]{1,0:T(8,128)(2,1)}, bf16[128,64]{1,0:T(8,128)(2,1)}, ...), branch_computations={%region_3.3_spmd, %region_4.4_spmd} | conditional | flops 143152128 | bytes 10310676 | solution.py:94
  228.9 10.8 %all_gather.21 = bf16[16,4096]{1,0:T(8,128)(2,1)S(1)} all-gather(bf16[16,1024]{1,0:T(8,128)(2,1)} %copy-done.2), channel_id=1, replica_groups=mesh['section'=2,'dp'=4,'tensor'=4] {'tensor'}, dimensions={1}, use_global_device_ids=true | all-gather | bytes 163840 | tf_op jit(solution)/shard_map/while/body/eval_jaxpr/all_gather | solution.py:100
  252.2 7.4 %conditional.6 = (bf16[16,1024]{1,0:T(8,128)(2,1)S(1)}, f32[64,64]{1,0:T(8,128)}) conditional(s32[]{:T(128)} %convert_element_type.136, f32[64,64]{1,0:T(8,128)} %get-tuple-element.548, (bf16[16,4096]{1,0:T(8,128)(2,1)S(1)}, f32[128,4096]{1,0:T(8,128)S(1)}, s32[]{:T(128)}, bf16[1024,4096]{1,0:T(8,128)(2,1)}, bf16[128,64]{1,0:T(8,128)(2,1)}, ...), branch_computations={%region_3.3_spmd, %region_4.4_spmd} | conditional | flops 143152128 | bytes 10310676 | solution.py:94
  260.2 10.7 %all_gather.21 = bf16[16,4096]{1,0:T(8,128)(2,1)S(1)} all-gather(bf16[16,1024]{1,0:T(8,128)(2,1)} %copy-done.2), channel_id=1, replica_groups=mesh['section'=2,'dp'=4,'tensor'=4] {'tensor'}, dimensions={1}, use_global_device_ids=true | all-gather | bytes 163840 | tf_op jit(solution)/shard_map/while/body/eval_jaxpr/all_gather | solution.py:100
  283.5 7.4 %conditional.6 = (bf16[16,1024]{1,0:T(8,128)(2,1)S(1)}, f32[64,64]{1,0:T(8,128)}) conditional(s32[]{:T(128)} %convert_element_type.136, f32[64,64]{1,0:T(8,128)} %get-tuple-element.548, (bf16[16,4096]{1,0:T(8,128)(2,1)S(1)}, f32[128,4096]{1,0:T(8,128)S(1)}, s32[]{:T(128)}, bf16[1024,4096]{1,0:T(8,128)(2,1)}, bf16[128,64]{1,0:T(8,128)(2,1)}, ...), branch_computations={%region_3.3_spmd, %region_4.4_spmd} | conditional | flops 143152128 | bytes 10310676 | solution.py:94
  291.5 10.7 %all_gather.21 = bf16[16,4096]{1,0:T(8,128)(2,1)S(1)} all-gather(bf16[16,1024]{1,0:T(8,128)(2,1)} %copy-done.2), channel_id=1, replica_groups=mesh['section'=2,'dp'=4,'tensor'=4] {'tensor'}, dimensions={1}, use_global_device_ids=true | all-gather | bytes 163840 | tf_op jit(solution)/shard_map/while/body/eval_jaxpr/all_gather | solution.py:100
  314.7 7.4 %conditional.6 = (bf16[16,1024]{1,0:T(8,128)(2,1)S(1)}, f32[64,64]{1,0:T(8,128)}) conditional(s32[]{:T(128)} %convert_element_type.136, f32[64,64]{1,0:T(8,128)} %get-tuple-element.548, (bf16[16,4096]{1,0:T(8,128)(2,1)S(1)}, f32[128,4096]{1,0:T(8,128)S(1)}, s32[]{:T(128)}, bf16[1024,4096]{1,0:T(8,128)(2,1)}, bf16[128,64]{1,0:T(8,128)(2,1)}, ...), branch_computations={%region_3.3_spmd, %region_4.4_spmd} | conditional | flops 143152128 | bytes 10310676 | solution.py:94
  322.8 10.7 %all_gather.21 = bf16[16,4096]{1,0:T(8,128)(2,1)S(1)} all-gather(bf16[16,1024]{1,0:T(8,128)(2,1)} %copy-done.2), channel_id=1, replica_groups=mesh['section'=2,'dp'=4,'tensor'=4] {'tensor'}, dimensions={1}, use_global_device_ids=true | all-gather | bytes 163840 | tf_op jit(solution)/shard_map/while/body/eval_jaxpr/all_gather | solution.py:100
  345.9 7.4 %conditional.6 = (bf16[16,1024]{1,0:T(8,128)(2,1)S(1)}, f32[64,64]{1,0:T(8,128)}) conditional(s32[]{:T(128)} %convert_element_type.136, f32[64,64]{1,0:T(8,128)} %get-tuple-element.548, (bf16[16,4096]{1,0:T(8,128)(2,1)S(1)}, f32[128,4096]{1,0:T(8,128)S(1)}, s32[]{:T(128)}, bf16[1024,4096]{1,0:T(8,128)(2,1)}, bf16[128,64]{1,0:T(8,128)(2,1)}, ...), branch_computations={%region_3.3_spmd, %region_4.4_spmd} | conditional | flops 143152128 | bytes 10310676 | solution.py:94
  354.0 10.7 %all_gather.21 = bf16[16,4096]{1,0:T(8,128)(2,1)S(1)} all-gather(bf16[16,1024]{1,0:T(8,128)(2,1)} %copy-done.2), channel_id=1, replica_groups=mesh['section'=2,'dp'=4,'tensor'=4] {'tensor'}, dimensions={1}, use_global_device_ids=true | all-gather | bytes 163840 | tf_op jit(solution)/shard_map/while/body/eval_jaxpr/all_gather | solution.py:100
  377.2 7.4 %conditional.6 = (bf16[16,1024]{1,0:T(8,128)(2,1)S(1)}, f32[64,64]{1,0:T(8,128)}) conditional(s32[]{:T(128)} %convert_element_type.136, f32[64,64]{1,0:T(8,128)} %get-tuple-element.548, (bf16[16,4096]{1,0:T(8,128)(2,1)S(1)}, f32[128,4096]{1,0:T(8,128)S(1)}, s32[]{:T(128)}, bf16[1024,4096]{1,0:T(8,128)(2,1)}, bf16[128,64]{1,0:T(8,128)(2,1)}, ...), branch_computations={%region_3.3_spmd, %region_4.4_spmd} | conditional | flops 143152128 | bytes 10310676 | solution.py:94
  385.2 10.7 %all_gather.21 = bf16[16,4096]{1,0:T(8,128)(2,1)S(1)} all-gather(bf16[16,1024]{1,0:T(8,128)(2,1)} %copy-done.2), channel_id=1, replica_groups=mesh['section'=2,'dp'=4,'tensor'=4] {'tensor'}, dimensions={1}, use_global_device_ids=true | all-gather | bytes 163840 | tf_op jit(solution)/shard_map/while/body/eval_jaxpr/all_gather | solution.py:100
  408.4 7.4 %conditional.6 = (bf16[16,1024]{1,0:T(8,128)(2,1)S(1)}, f32[64,64]{1,0:T(8,128)}) conditional(s32[]{:T(128)} %convert_element_type.136, f32[64,64]{1,0:T(8,128)} %get-tuple-element.548, (bf16[16,4096]{1,0:T(8,128)(2,1)S(1)}, f32[128,4096]{1,0:T(8,128)S(1)}, s32[]{:T(128)}, bf16[1024,4096]{1,0:T(8,128)(2,1)}, bf16[128,64]{1,0:T(8,128)(2,1)}, ...), branch_computations={%region_3.3_spmd, %region_4.4_spmd} | conditional | flops 143152128 | bytes 10310676 | solution.py:94
  416.4 10.7 %all_gather.21 = bf16[16,4096]{1,0:T(8,128)(2,1)S(1)} all-gather(bf16[16,1024]{1,0:T(8,128)(2,1)} %copy-done.2), channel_id=1, replica_groups=mesh['section'=2,'dp'=4,'tensor'=4] {'tensor'}, dimensions={1}, use_global_device_ids=true | all-gather | bytes 163840 | tf_op jit(solution)/shard_map/while/body/eval_jaxpr/all_gather | solution.py:100
  440.3 10.8 %all_gather.21 = bf16[16,4096]{1,0:T(8,128)(2,1)S(1)} all-gather(bf16[16,1024]{1,0:T(8,128)(2,1)} %copy-done.2), channel_id=1, replica_groups=mesh['section'=2,'dp'=4,'tensor'=4] {'tensor'}, dimensions={1}, use_global_device_ids=true | all-gather | bytes 163840 | tf_op jit(solution)/shard_map/while/body/eval_jaxpr/all_gather | solution.py:100
  451.1 15.3 %collective-permute-start = (bf16[16,4096]{1,0:T(8,128)(2,1)S(1)}, bf16[16,4096]{1,0:T(8,128)(2,1)S(1)}, u32[]{:S(2)}, u32[]{:S(2)}) collective-permute-start(bf16[16,4096]{1,0:T(8,128)(2,1)S(1)} %get-tuple-element.588), channel_id=1, source_target_pairs={{16,0},{17,1},{18,2},{19,3},{20,4},{21,5},{22,6},{23,7},{24,8},{25... | collective-permute-start | bytes 393224 | tf_op jit(solution)/shard_map/while/body/eval_jaxpr/ppermute | solution.py:16
  468.8 8.0 %psum.14 = f32[2,1024]{1,0:T(2,128)S(1)} all-reduce(f32[2,1024]{1,0:T(2,128)S(1)} %broadcast_multiply_fusion.1), channel_id=1, replica_groups=mesh['section'=2,'dp'=4,'tensor'=4] {'dp'}, use_global_device_ids=true, to_apply=%region_9.10 | all-reduce | flops 2048 | bytes 16384 | tf_op jit(solution)/shard_map/psum | solution.py:130
  477.0 17.0 %psum.15 = f32[2,64]{1,0:T(2,128)} all-reduce(f32[2,64]{1,0:T(2,128)S(1)} %fusion.32), channel_id=1, replica_groups=mesh['section'=2,'dp'=4,'tensor'=4] {'section','tensor'}, use_global_device_ids=true, to_apply=%region_10.11 | all-reduce | flops 128 | bytes 1024 | tf_op jit(solution)/shard_map/psum | solution.py:133
  (148 shorter events, 201.6 us)
Async XLA Ops:
  7.2 469.7 %copy-start = (bf16[1,64,1024]{2,1,0:T(8,128)(2,1)S(1)}, bf16[1,64,1024]{2,1,0:T(8,128)(2,1)}, u32[]{:S(2)}) copy-start(bf16[1,64,1024]{2,1,0:T(8,128)(2,1)} %param.17) | copy-start | bytes 393220
  7.2 1.3 copy-start.1
  7.2 2.1 copy-start.3
  7.2 92.1 %all-gather.5.cloned.1.call-start = ((), (), s32[]{:S(2)}) async-start(), calls=%async_computation | async-start | bytes 10485760 | tf_op jit(solution)/shard_map/all_gather | solution.py:52
  7.9 177.9 %all-gather.7.cloned.1.call-start = ((), (), s32[]{:S(2)}) async-start(), calls=%async_computation.1 | async-start | bytes 5242880 | tf_op jit(solution)/shard_map/all_gather | solution.py:55
  99.3 5.7 %copy-start.7 = (s32[1,2]{1,0:T(1,128)S(1)}, s32[1,2]{1,0:T(1,128)}, u32[]{:S(2)}) copy-start(s32[1,2]{1,0:T(1,128)} %param.15) | copy-start | bytes 28
  106.8 1.4 copy-start.6
  106.8 1.4 copy-start.4
  201.0 0.6 copy-start.2
  215.3 2.3 collective-permute-start
  228.3 0.6 copy-start.2
  242.6 6.3 %collective-permute-start = (bf16[16,4096]{1,0:T(8,128)(2,1)S(1)}, bf16[16,4096]{1,0:T(8,128)(2,1)S(1)}, u32[]{:S(2)}, u32[]{:S(2)}) collective-permute-start(bf16[16,4096]{1,0:T(8,128)(2,1)S(1)} %get-tuple-element.588), channel_id=1, source_target_pairs={{16,0},{17,1},{18,2},{19,3},{20,4},{21,5},{22,6},{23,7},{24,8},{25... | collective-permute-start | bytes 393224 | tf_op jit(solution)/shard_map/while/body/eval_jaxpr/ppermute | solution.py:16
  259.6 0.6 copy-start.2
  273.9 6.2 %collective-permute-start = (bf16[16,4096]{1,0:T(8,128)(2,1)S(1)}, bf16[16,4096]{1,0:T(8,128)(2,1)S(1)}, u32[]{:S(2)}, u32[]{:S(2)}) collective-permute-start(bf16[16,4096]{1,0:T(8,128)(2,1)S(1)} %get-tuple-element.588), channel_id=1, source_target_pairs={{16,0},{17,1},{18,2},{19,3},{20,4},{21,5},{22,6},{23,7},{24,8},{25... | collective-permute-start | bytes 393224 | tf_op jit(solution)/shard_map/while/body/eval_jaxpr/ppermute | solution.py:16
  290.9 0.6 copy-start.2
  305.2 6.2 %collective-permute-start = (bf16[16,4096]{1,0:T(8,128)(2,1)S(1)}, bf16[16,4096]{1,0:T(8,128)(2,1)S(1)}, u32[]{:S(2)}, u32[]{:S(2)}) collective-permute-start(bf16[16,4096]{1,0:T(8,128)(2,1)S(1)} %get-tuple-element.588), channel_id=1, source_target_pairs={{16,0},{17,1},{18,2},{19,3},{20,4},{21,5},{22,6},{23,7},{24,8},{25... | collective-permute-start | bytes 393224 | tf_op jit(solution)/shard_map/while/body/eval_jaxpr/ppermute | solution.py:16
  322.2 0.6 copy-start.2
  336.4 6.2 %collective-permute-start = (bf16[16,4096]{1,0:T(8,128)(2,1)S(1)}, bf16[16,4096]{1,0:T(8,128)(2,1)S(1)}, u32[]{:S(2)}, u32[]{:S(2)}) collective-permute-start(bf16[16,4096]{1,0:T(8,128)(2,1)S(1)} %get-tuple-element.588), channel_id=1, source_target_pairs={{16,0},{17,1},{18,2},{19,3},{20,4},{21,5},{22,6},{23,7},{24,8},{25... | collective-permute-start | bytes 393224 | tf_op jit(solution)/shard_map/while/body/eval_jaxpr/ppermute | solution.py:16
  367.6 6.2 %collective-permute-start = (bf16[16,4096]{1,0:T(8,128)(2,1)S(1)}, bf16[16,4096]{1,0:T(8,128)(2,1)S(1)}, u32[]{:S(2)}, u32[]{:S(2)}) collective-permute-start(bf16[16,4096]{1,0:T(8,128)(2,1)S(1)} %get-tuple-element.588), channel_id=1, source_target_pairs={{16,0},{17,1},{18,2},{19,3},{20,4},{21,5},{22,6},{23,7},{24,8},{25... | collective-permute-start | bytes 393224 | tf_op jit(solution)/shard_map/while/body/eval_jaxpr/ppermute | solution.py:16
  398.9 6.2 %collective-permute-start = (bf16[16,4096]{1,0:T(8,128)(2,1)S(1)}, bf16[16,4096]{1,0:T(8,128)(2,1)S(1)}, u32[]{:S(2)}, u32[]{:S(2)}) collective-permute-start(bf16[16,4096]{1,0:T(8,128)(2,1)S(1)} %get-tuple-element.588), channel_id=1, source_target_pairs={{16,0},{17,1},{18,2},{19,3},{20,4},{21,5},{22,6},{23,7},{24,8},{25... | collective-permute-start | bytes 393224 | tf_op jit(solution)/shard_map/while/body/eval_jaxpr/ppermute | solution.py:16
  430.0 6.3 %collective-permute-start = (bf16[16,4096]{1,0:T(8,128)(2,1)S(1)}, bf16[16,4096]{1,0:T(8,128)(2,1)S(1)}, u32[]{:S(2)}, u32[]{:S(2)}) collective-permute-start(bf16[16,4096]{1,0:T(8,128)(2,1)S(1)} %get-tuple-element.588), channel_id=1, source_target_pairs={{16,0},{17,1},{18,2},{19,3},{20,4},{21,5},{22,6},{23,7},{24,8},{25... | collective-permute-start | bytes 393224 | tf_op jit(solution)/shard_map/while/body/eval_jaxpr/ppermute | solution.py:16
  439.7 0.6 copy-start.2
  451.1 16.3 %collective-permute-start = (bf16[16,4096]{1,0:T(8,128)(2,1)S(1)}, bf16[16,4096]{1,0:T(8,128)(2,1)S(1)}, u32[]{:S(2)}, u32[]{:S(2)}) collective-permute-start(bf16[16,4096]{1,0:T(8,128)(2,1)S(1)} %get-tuple-element.588), channel_id=1, source_target_pairs={{16,0},{17,1},{18,2},{19,3},{20,4},{21,5},{22,6},{23,7},{24,8},{25... | collective-permute-start | bytes 393224 | tf_op jit(solution)/shard_map/while/body/eval_jaxpr/ppermute | solution.py:16
  476.9 17.2 %copy-start.5 = (f32[2,1024]{1,0:T(2,128)}, f32[2,1024]{1,0:T(2,128)S(1)}, u32[]{:S(2)}) copy-start(f32[2,1024]{1,0:T(2,128)S(1)} %psum.14) | copy-start | bytes 24580
  (3 other events, 1.8 us)
Sparse Core Ops, SparseCore 0:
  9.9 89.3 all-gather.4
  105.1 80.7 all-gather.6
